TPU v7x, 512 devices: a whole 4x4x16 slice. The times are simulated.
512 devices in a mesh: gx: 16 (over y, x_lo, core), gy: 32 (over z, x_hi).
Axes of the slice: x: 4 (x_hi: 2, x_lo: 2; x = x_hi * 2 + x_lo), y: 4, z: 16, core: 2. Of those that a mesh axis runs over, the one named last changes fastest.
Arguments:
- site_tensors: bfloat16 [128, 64, 256, 256], P('gx', 'gy'), may hold values from -6 to 6
- test_matrix: bfloat16 [128, 64, 16, 256], P('gx', 'gy'), may hold values from -0.375 to 0.375
Outputs:
- coarse: bfloat16 [64, 64, 256, 256], P('gx', 'gy')
- log_norm: float32 [64, 64], P('gx', 'gy')
- trace: float32 [64, 64], P('gx', 'gy')
All inputs are finite; a program needn't handle non-finite values.
Results may differ from a plain program's by a relative error of at most 0.0086.
Values may be sent and summed in bfloat16 or wider, within the bound.
No kernel may reach another device: no remote copies, remote signals or barrier semaphores. Data moves between devices by JAX's collectives and lax.ppermute only.
A program may use at most 64 MiB of HBM per device.

v0:
```python
import jax
import jax.numpy as jnp
from jax import lax
from jax.sharding import PartitionSpec as P

CHI = 16


def from_behind(x, axis, by):
    length = lax.axis_size(axis)
    return lax.ppermute(x, axis, [(i, (i + by) % length) for i in range(length)])


def split_block(tensors, tests):
    width_count = tensors.shape[0]
    height_count = tensors.shape[1]
    count = width_count * height_count
    flat_tensors = tensors.reshape(count, CHI * CHI, CHI * CHI)
    flat_tests = tests.reshape(count, CHI, CHI * CHI)
    sketch = jnp.einsum(
        "sij,skj->sik", flat_tensors, flat_tests, preferred_element_type=jnp.float32
    )
    gram_matrix = jnp.einsum("sik,sil->skl", sketch, sketch, precision=lax.Precision.HIGHEST)
    lower_factor = jnp.linalg.cholesky(gram_matrix)
    basis = jax.scipy.linalg.solve_triangular(
        lower_factor, jnp.swapaxes(sketch, 1, 2), lower=True
    ).astype(jnp.bfloat16)
    second = jnp.einsum(
        "ski,sij->skj", basis, flat_tensors, preferred_element_type=jnp.float32
    ).astype(jnp.bfloat16)
    shape_out = (width_count, height_count, CHI, CHI * CHI)
    return (basis.reshape(shape_out), second.reshape(shape_out))


def pick_sites(field):
    width_count = field.shape[0]
    height_count = field.shape[1]
    grid = field.reshape(width_count // 2, 2, height_count // 2, 2, CHI, CHI * CHI)
    chosen = jnp.stack([grid[:, 0, :, 0], grid[:, 1, :, 1]], axis=2)
    return chosen.reshape(width_count // 2 * height_count, CHI, CHI * CHI)


def contract_sites(north_east, north_west, south_east, south_west):
    count = north_east.shape[0]
    width = CHI * CHI
    low_left = north_east.reshape(count, CHI, CHI, CHI)
    low_right = north_west.reshape(count, CHI, CHI, CHI)
    high_left = south_east.reshape(count, CHI, CHI, CHI)
    high_right = south_west.reshape(count, CHI, CHI, CHI)
    pair_low = jnp.einsum(
        "naur,nbvr->nabuv", low_left, low_right, preferred_element_type=jnp.float32
    ).astype(jnp.bfloat16)
    pair_high = jnp.einsum(
        "ncru,nevr->nceuv", high_left, high_right, preferred_element_type=jnp.float32
    ).astype(jnp.bfloat16)
    pair_low = pair_low.reshape(count, width, width)
    pair_high = pair_high.reshape(count, width, width)
    raw = jnp.einsum("nij,nkj->nik", pair_low, pair_high, preferred_element_type=jnp.float32)
    squares = jnp.sum(raw * raw, axis=(1, 2))
    norm_value = jnp.sqrt(squares + 1e-06)
    row_index = lax.broadcasted_iota(jnp.int32, (width, width), 0)
    col_index = lax.broadcasted_iota(jnp.int32, (width, width), 1)
    trace_mask = (
        (col_index // CHI == row_index % CHI) & (col_index % CHI == row_index // CHI)
    ).astype(jnp.float32)
    traced = jnp.sum(raw * trace_mask[None], axis=(1, 2))
    coarse = (CHI * CHI * raw / norm_value[:, None, None]).astype(jnp.bfloat16)
    return (coarse, jnp.log(norm_value), CHI * traced / norm_value)


def body(site_tensors, test_matrix):
    width_count = site_tensors.shape[0]
    height_count = site_tensors.shape[1]
    column_in = from_behind((site_tensors[0:1], test_matrix[0:1]), "gx", -1)
    wider_tensors = jnp.concatenate([site_tensors, column_in[0]], axis=0)
    wider_tests = jnp.concatenate([test_matrix, column_in[1]], axis=0)
    row_in = from_behind((wider_tensors[:, 0:1], wider_tests[:, 0:1]), "gy", -1)
    block_tensors = jnp.concatenate([wider_tensors, row_in[0]], axis=1)
    block_tests = jnp.concatenate([wider_tests, row_in[1]], axis=1)
    basis_all, second_all = split_block(block_tensors, block_tests)
    north_east = pick_sites(basis_all[:width_count, :height_count])
    north_west = pick_sites(basis_all[1:, :height_count])
    south_east = pick_sites(second_all[:width_count, 1:])
    south_west = pick_sites(second_all[1:, 1:])
    coarse, log_norm, trace = contract_sites(north_east, north_west, south_east, south_west)
    half_width = width_count // 2
    coarse = coarse.reshape(half_width, height_count, CHI * CHI, CHI * CHI)
    return (
        coarse,
        log_norm.reshape(half_width, height_count),
        trace.reshape(half_width, height_count),
    )


def solution(mesh):
    in_specs = (P("gx", "gy", None, None), P("gx", "gy", None, None))
    out_specs = (P("gx", "gy", None, None), P("gx", "gy"), P("gx", "gy"))
    return jax.shard_map(body, mesh=mesh, in_specs=in_specs, out_specs=out_specs, check_vma=False)
```

profile of v0, /device:TPU:1, one launch (start us, length us, event | category | flops | bytes accessed | tf_op | source)
XLA Modules:
  0.0 204.6 jit_solution(18243714266222912376)
XLA Ops:
  0.6 1.0 slice.60
  1.6 8.8 %collective-permute-start = (bf16[1,2,256,256]{3,2,1,0:T(8,128)(2,1)S(1)}, bf16[1,2,256,256]{3,2,1,0:T(8,128)(2,1)S(1)}, u32[]{:S(2)}, u32[]{:S(2)}) collective-permute-start(bf16[1,2,256,256]{3,2,1,0:T(8,128)(2,1)S(1)} %slice.60), channel_id=1, source_target_pairs={{0,480},{32,0},{64,32},{96,64},{128,96},{160,128},{192,160},{224,1... | collective-permute-start | bytes 786440 | tf_op jit(solution)/shard_map/ppermute | solution.py:11
  10.4 1.8 constant_dynamic-update-slice_fusion.1
  12.2 0.0 copy-start.4
  12.2 0.0 collective-permute-done
  12.2 0.1 slice.76
  12.3 11.5 %collective-permute-start.1 = (bf16[9,1,256,256]{3,2,1,0:T(8,128)(2,1)S(1)}, bf16[9,1,256,256]{3,2,1,0:T(8,128)(2,1)S(1)}, u32[]{:S(2)}, u32[]{:S(2)}) collective-permute-start(bf16[9,1,256,256]{3,2,1,0:T(8,128)(2,1)S(1)} %slice.76), channel_id=1, source_target_pairs={{0,31},{1,0},{2,1},{3,2},{4,3},{5,4},{6,5},{7,6},{8,7},{9,8},{10,9... | collective-permute-start | bytes 3538952 | tf_op jit(solution)/shard_map/ppermute | solution.py:11
  23.8 0.0 copy-done.4
  23.8 4.0 %collective-permute-start.2 = (bf16[1,2,16,256]{3,2,1,0:T(8,128)(2,1)S(1)}, bf16[1,2,16,256]{3,2,1,0:T(8,128)(2,1)S(1)}, u32[]{:S(2)}, u32[]{:S(2)}) collective-permute-start(bf16[1,2,16,256]{3,2,1,0:T(8,128)(2,1)S(1)} %slice.62), channel_id=1, source_target_pairs={{0,480},{32,0},{64,32},{96,64},{128,96},{160,128},{192,160},{224,1... | collective-permute-start | bytes 49160 | tf_op jit(solution)/shard_map/ppermute | solution.py:11
  28.0 1.0 fusion.5
  28.9 0.6 iota_compare_fusion
  29.5 12.8 %collective-permute-done.2 = bf16[1,2,16,256]{3,2,1,0:T(8,128)(2,1)S(1)} collective-permute-done((bf16[1,2,16,256]{3,2,1,0:T(8,128)(2,1)S(1)}, bf16[1,2,16,256]{3,2,1,0:T(8,128)(2,1)S(1)}, u32[]{:S(2)}, u32[]{:S(2)}) %collective-permute-start.2) | collective-permute-done | bytes 16416 | tf_op jit(solution)/shard_map/ppermute | solution.py:11
  42.3 9.9 %collective-permute-start.3 = (bf16[9,1,16,256]{3,2,1,0:T(8,128)(2,1)S(1)}, bf16[9,1,16,256]{3,2,1,0:T(8,128)(2,1)S(1)}, u32[]{:S(2)}, u32[]{:S(2)}) collective-permute-start(bf16[9,1,16,256]{3,2,1,0:T(8,128)(2,1)S(1)} %slice.77), channel_id=1, source_target_pairs={{0,31},{1,0},{2,1},{3,2},{4,3},{5,4},{6,5},{7,6},{8,7},{9,8},{10,9... | collective-permute-start | bytes 221192 | tf_op jit(solution)/shard_map/ppermute | solution.py:11
  52.2 0.6 iota_compare_fusion.1
  52.8 0.8 collective-permute-done.3
  53.6 0.0 collective-permute-done.1
  53.6 0.3 pad_maximum_fusion
  53.9 1.0 fusion.13
  54.9 0.0 copy-start
  54.9 0.8 copy-done
  55.7 1.2 fusion.14
  56.9 1.7 copy.60
  58.7 1.8 fusion.7
  60.5 40.9 %custom-call.8 = f32[27,16,16]{2,1,0:T(8,128)} custom-call(f32[27,16,16]{2,1,0:T(8,128)} %fusion.7), custom_call_target="Cholesky" | custom-call | tf_op jit(solution)/shard_map/jit(cholesky)/cholesky | solution.py:24
  101.4 1.0 select_reduce_fusion
  102.3 0.7 copy.61
  103.0 0.7 compare_reduce_fusion
  103.7 1.7 select_bitcast_fusion
  105.5 34.8 %custom-call.9 = f32[27,1,16,16]{2,3,1,0:T(8,128)} custom-call(f32[27,1,16,16]{3,2,1,0:T(8,128)} %select_bitcast_fusion), custom_call_target="InvertDiagBlocksLowerTriangular" | custom-call | tf_op jit(solution)/shard_map/jit(_solve_triangular)/vmap()/triangular_solve | solution.py:25
  140.3 1.7 convolution_convert_fusion.1
  142.0 0.0 copy-start.1
  142.0 0.6 convolution_convert_fusion
  142.6 0.1 copy-done.1
  142.7 0.4 reshape.239
  143.1 0.4 reshape.240
  143.5 5.6 %convert_bitcast_fusion = bf16[8,16,16,16,16]{3,4,1,2,0:T(8,128)(2,1)} fusion(bf16[8,16,16,16,1]{3,2,1,0,4:T(8,128)(2,1)S(1)} %reshape.240, bf16[8,16,16,16,1]{3,2,1,0,4:T(8,128)(2,1)S(1)} %reshape.239), kind=kOutput, calls=%fused_computation | convolution fusion | flops 17301504 | bytes 1179648 | tf_op jit(solution)/shard_map/ncru,nevr->nceuv/dot_general | solution.py:53
  149.1 11.4 %copy.73 = bf16[8,16,16,16,16]{4,3,2,1,0:T(8,128)(2,1)} copy(bf16[8,16,16,16,16]{3,4,1,2,0:T(8,128)(2,1)} %convert_bitcast_fusion) | data formatting | bytes 2097152 | tf_op jit(solution)/shard_map/convert_element_type | solution.py:55
  160.5 0.0 copy-start.2
  160.5 10.1 %reshape.235 = bf16[8,256,256]{2,1,0:T(8,128)(2,1)S(1)} reshape(bf16[8,16,16,16,16]{4,3,2,1,0:T(8,128)(2,1)} %copy.73) | data formatting | bytes 2097152 | tf_op jit(solution)/shard_map/reshape | solution.py:57
  170.6 0.0 copy-done.2
  170.7 0.4 reshape.237
  171.1 0.4 reshape.238
  171.5 5.6 %convert_bitcast_fusion.1 = bf16[8,16,16,16,16]{3,4,1,2,0:T(8,128)(2,1)} fusion(bf16[8,16,16,16,1]{3,2,1,0,4:T(8,128)(2,1)S(1)} %reshape.238, bf16[8,16,16,16,1]{3,2,1,0,4:T(8,128)(2,1)S(1)} %reshape.237), kind=kOutput, calls=%fused_computation.1 | convolution fusion | flops 17301504 | bytes 1179648 | tf_op jit(solution)/shard_map/naur,nbvr->nabuv/dot_general | solution.py:50
  177.1 11.4 %copy.68 = bf16[8,16,16,16,16]{4,3,2,1,0:T(8,128)(2,1)} copy(bf16[8,16,16,16,16]{3,4,1,2,0:T(8,128)(2,1)} %convert_bitcast_fusion.1) | data formatting | bytes 2097152 | tf_op jit(solution)/shard_map/convert_element_type | solution.py:52
  188.5 0.0 copy-start.3
  188.5 11.1 %reshape.231 = bf16[8,256,256]{2,1,0:T(8,128)(2,1)} reshape(bf16[8,16,16,16,16]{4,3,2,1,0:T(8,128)(2,1)} %copy.68) | data formatting | bytes 2097152 | tf_op jit(solution)/shard_map/reshape | solution.py:56
  199.6 0.0 copy-done.3
  199.6 1.8 multiply_reduce_fusion
  201.4 0.1 log.15
  201.5 0.7 copy.74
  202.1 0.1 div.41
  202.2 0.7 copy.75
  202.9 1.7 divide_convert_fusion
  (20 shorter events, 0.2 us)
Async XLA Ops:
  1.6 10.6 %collective-permute-start = (bf16[1,2,256,256]{3,2,1,0:T(8,128)(2,1)S(1)}, bf16[1,2,256,256]{3,2,1,0:T(8,128)(2,1)S(1)}, u32[]{:S(2)}, u32[]{:S(2)}) collective-permute-start(bf16[1,2,256,256]{3,2,1,0:T(8,128)(2,1)S(1)} %slice.60), channel_id=1, source_target_pairs={{0,480},{32,0},{64,32},{96,64},{128,96},{160,128},{192,160},{224,1... | collective-permute-start | bytes 786440 | tf_op jit(solution)/shard_map/ppermute | solution.py:11
  12.2 11.6 %copy-start.4 = (bf16[8,2,16,256]{3,2,1,0:T(8,128)(2,1)S(1)}, bf16[8,2,16,256]{3,2,1,0:T(8,128)(2,1)}, u32[]{:S(2)}) copy-start(bf16[8,2,16,256]{3,2,1,0:T(8,128)(2,1)} %param.3) | copy-start | bytes 393220
  12.3 41.3 %collective-permute-start.1 = (bf16[9,1,256,256]{3,2,1,0:T(8,128)(2,1)S(1)}, bf16[9,1,256,256]{3,2,1,0:T(8,128)(2,1)S(1)}, u32[]{:S(2)}, u32[]{:S(2)}) collective-permute-start(bf16[9,1,256,256]{3,2,1,0:T(8,128)(2,1)S(1)} %slice.76), channel_id=1, source_target_pairs={{0,31},{1,0},{2,1},{3,2},{4,3},{5,4},{6,5},{7,6},{8,7},{9,8},{10,9... | collective-permute-start | bytes 3538952 | tf_op jit(solution)/shard_map/ppermute | solution.py:11
  23.8 18.4 %collective-permute-start.2 = (bf16[1,2,16,256]{3,2,1,0:T(8,128)(2,1)S(1)}, bf16[1,2,16,256]{3,2,1,0:T(8,128)(2,1)S(1)}, u32[]{:S(2)}, u32[]{:S(2)}) collective-permute-start(bf16[1,2,16,256]{3,2,1,0:T(8,128)(2,1)S(1)} %slice.62), channel_id=1, source_target_pairs={{0,480},{32,0},{64,32},{96,64},{128,96},{160,128},{192,160},{224,1... | collective-permute-start | bytes 49160 | tf_op jit(solution)/shard_map/ppermute | solution.py:11
  42.3 11.3 %collective-permute-start.3 = (bf16[9,1,16,256]{3,2,1,0:T(8,128)(2,1)S(1)}, bf16[9,1,16,256]{3,2,1,0:T(8,128)(2,1)S(1)}, u32[]{:S(2)}, u32[]{:S(2)}) collective-permute-start(bf16[9,1,16,256]{3,2,1,0:T(8,128)(2,1)S(1)} %slice.77), channel_id=1, source_target_pairs={{0,31},{1,0},{2,1},{3,2},{4,3},{5,4},{6,5},{7,6},{8,7},{9,8},{10,9... | collective-permute-start | bytes 221192 | tf_op jit(solution)/shard_map/ppermute | solution.py:11
  54.9 0.8 copy-start
  142.0 0.7 copy-start.1
  160.5 10.1 %copy-start.2 = (bf16[27,16,256]{2,1,0:T(8,128)(2,1)S(1)}, bf16[27,16,256]{2,1,0:T(8,128)(2,1)}, u32[]{:S(2)}) copy-start(bf16[27,16,256]{2,1,0:T(8,128)(2,1)} %copy-done.1) | copy-start | bytes 663556
  188.5 11.1 %copy-start.3 = (f32[256,256]{1,0:T(8,128)S(1)}, f32[256,256]{1,0:T(8,128)}, u32[]{:S(2)}) copy-start(f32[256,256]{1,0:T(8,128)} %fusion.5) | copy-start | bytes 786436
where the time goes:
time: 206 us; the launch traced here: 205 us
  other arithmetic  85.2 us (41%)
  local copies, waits for them, and re-layouts  53.2 us (26%)
  starting transfers between devices  34.2 us (17%)
  matrix products  17.5 us (8%)
  waiting for transfers between devices  13.6 us (7%)
    another operation x4, other arithmetic, split_block(): lower_factor = jnp.linalg.cholesky(gram_matrix)  43.2 us
    another operation x3, other arithmetic, split_block(): jax.scipy.linalg.solve_triangular(lower_factor, jnp.swapaxes(sketch, 1, 2...  37.1 us
    ppermute x4, starting transfers between devices, from_behind(): lax.ppermute(x, axis, [(i, (i + by) % length) for i in range(length)])  34.2 us
    ppermute x4, waiting for transfers between devices, from_behind(): lax.ppermute(x, axis, [(i, (i + by) % length) for i in range(length)])  13.6 us
    convert_element_type x1, local copies, waits for them, and re-layouts, contract_sites(): pair_high = jnp.einsum('ncru,nevr->nceuv', high_left, high_right, preferr...  11.4 us
    convert_element_type x1, local copies, waits for them, and re-layouts, contract_sites(): pair_low = jnp.einsum('naur,nbvr->nabuv', low_left, low_right, preferred_...  11.4 us
    reshape x1, local copies, waits for them, and re-layouts, contract_sites(): pair_low = pair_low.reshape(count, width, width)  11.1 us
    reshape x1, local copies, waits for them, and re-layouts, contract_sites(): pair_high = pair_high.reshape(count, width, width)  10.1 us
  transfers between devices with their start and end apart: 4, of which 2 were waited for; matrix products, arithmetic and copies ran while one was open for 2% of the time, Pallas kernels for 0%

commit v1 on v0

v1 whole, which is shorter than its diff:
```python
import jax
import jax.numpy as jnp
from jax import lax
from jax.experimental import pallas as pl
from jax.experimental.pallas import tpu as pltpu
from jax.sharding import PartitionSpec as P

CHI = 16
WIDE = CHI * CHI
HALF = 128
NT = (((1,), (1,)), ((), ()))
NN = (((1,), (0,)), ((), ()))


def dot(a, b, dims=NN):
    return lax.dot_general(a, b, dims, preferred_element_type=jnp.float32)


def split_kernel(columns, rows, tensors, tests, basis, second, above, right, corner, vm, vt, work, sem_m, sem_t):
    sites = columns * rows
    place = [(s // rows, s % rows) for s in range(sites)]
    test_copy = pltpu.make_async_copy(tests, vt, sem_t)
    test_copy.start()
    copies = [pltpu.make_async_copy(tensors.at[x, y], vm.at[s], sem_m.at[s]) for s, (x, y) in enumerate(place)]
    for copy in copies:
        copy.start()
    test_copy.wait()
    for s, (x, y) in enumerate(place):
        copies[s].wait()
        sketch = dot(vt[x, y], vm[s], NT)
        for h in range(2):
            work[h, pl.ds(s, CHI, stride=sites), :] = sketch[:, h * HALF : (h + 1) * HALF]

    def line(h, k):
        return work[h, k * sites : (k + 1) * sites, :]

    def inner(i, j):
        parts = line(0, i) * line(0, j) + line(1, i) * line(1, j)
        return jnp.broadcast_to(jnp.sum(parts, axis=1, keepdims=True), (sites, HALF))

    gram = {(i, j): inner(i, j) for j in range(CHI) for i in range(j, CHI)}
    for k in range(CHI):
        scale = lax.rsqrt(gram[k, k])
        lower = {i: gram[i, k] * scale for i in range(k + 1, CHI)}
        for i in range(k + 1, CHI):
            for j in range(k + 1, i + 1):
                gram[i, j] = gram[i, j] - lower[i] * lower[j]
        for h in range(2):
            row = line(h, k) * scale
            work[h, k * sites : (k + 1) * sites, :] = row
            for i in range(k + 1, CHI):
                work[h, i * sites : (i + 1) * sites, :] = line(h, i) - lower[i] * row
    for s, (x, y) in enumerate(place):
        rows_k = [work[h, pl.ds(s, CHI, stride=sites), :] for h in range(2)]
        q = jnp.concatenate(rows_k, axis=1).astype(jnp.bfloat16)
        rest = dot(q, vm[s]).astype(jnp.bfloat16)
        if y == 1 and x == 0:
            right[0] = q
        else:
            basis[x, y] = q
        if y == 1:
            second[x] = rest
        elif x == 0:
            corner[0] = rest
        else:
            above[x - 1] = rest


def split_block(tensors, tests):
    columns, rows = tensors.shape[0], tensors.shape[1]
    sites = columns * rows
    shapes = [(columns, rows), (columns,), (columns - 1,), (1,), (1,)]
    anywhere = pl.BlockSpec(memory_space=pl.ANY)
    return pl.pallas_call(
        lambda *refs: split_kernel(columns, rows, *refs),
        out_shape=[pltpu.VMEM(shape + (CHI, WIDE), jnp.bfloat16) for shape in shapes],
        in_specs=[anywhere] * 2,
        out_specs=[pl.BlockSpec(memory_space=pltpu.VMEM)] * 5,
        scratch_shapes=[
            pltpu.VMEM((sites, WIDE, WIDE), jnp.bfloat16),
            pltpu.VMEM((columns, rows, CHI, WIDE), jnp.bfloat16),
            pltpu.VMEM((2, CHI * sites, HALF), jnp.float32),
            pltpu.SemaphoreType.DMA((sites,)),
            pltpu.SemaphoreType.DMA,
        ],
        name="split",
    )(tensors, tests)


def widen(half, pick, tile):
    spread = jnp.broadcast_to(half.astype(jnp.float32)[:, None, :], (CHI, CHI, WIDE)).reshape(WIDE, WIDE)
    spread = jnp.where(pick, spread, 0.0).astype(jnp.bfloat16)
    return dot(spread, tile).astype(jnp.bfloat16)


def pair_up(wide, other, own, out):
    left = jnp.concatenate([other[:, :HALF], other[:, HALF:]], axis=0)
    for a in range(0, CHI, 2):
        blocks = []
        for step in range(2):
            piece = wide[(a + step) * CHI : (a + step + 1) * CHI, :]
            zero = jnp.zeros_like(piece)
            blocks.append(jnp.concatenate([jnp.where(own[v], piece, zero) for v in range(8)], axis=0))
        got = dot(left, jnp.concatenate(blocks, axis=1)).astype(jnp.bfloat16)
        for step in range(2):
            base = (a + step) * CHI
            for h in range(2):
                out[base : base + CHI, h * HALF : (h + 1) * HALF] = got[
                    h * CHI : (h + 1) * CHI, step * HALF : (step + 1) * HALF
                ]


def contract_kernel(count, row, *refs):
    coarse, logs, traces, low, high, done, sem = refs[-7:]
    if row:
        basis, above, right, corner, _, kept_logs, kept_traces = refs[:-7]
    else:
        basis, second = refs[:-7]

    def corners(p):
        if not row:
            return basis[2 * p, 0], basis[2 * p + 1, 0], second[2 * p], second[2 * p + 1]
        if p < count - 1:
            return basis[2 * p + 1, 1], basis[2 * p + 2, 1], above[2 * p], above[2 * p + 1]
        return basis[2 * p + 1, 1], right[0], above[2 * p], corner[0]

    iota = lambda shape, axis: lax.broadcasted_iota(jnp.int32, shape, axis)
    r, c = iota((WIDE, WIDE), 0), iota((WIDE, WIDE), 1)
    pick_minor = (c % CHI) == (r % CHI)
    pick_major = (c // CHI) == (r % CHI)
    rt, ct = iota((WIDE, HALF), 0), iota((WIDE, HALF), 1)
    tile_major = ((rt // CHI) == (ct % CHI)).astype(jnp.float32).astype(jnp.bfloat16)
    tile_minor = ((rt % CHI) == (ct % CHI)).astype(jnp.float32).astype(jnp.bfloat16)
    lane = iota((CHI, HALF), 1)
    own = [(lane // CHI) == v for v in range(8)]
    crossed = ((c // CHI) == (r % CHI)) & ((c % CHI) == (r // CHI))
    small_row, small_col = iota((2, count), 0), iota((2, count), 1)
    if row:
        all_logs, all_traces = kept_logs[...], kept_traces[...]
    else:
        all_logs = all_traces = jnp.zeros((2, count), jnp.float32)
    copies = []
    for p in range(count):
        north_east, north_west, south_east, south_west = corners(p)
        pair_up(widen(north_east, pick_minor, tile_major), north_west, own, low.at[p % 2])
        pair_up(widen(south_east, pick_major, tile_minor), south_west, own, high.at[p % 2])
        raw = dot(low[p % 2], high[p % 2], NT)
        square = jnp.sum(jnp.sum(raw * raw, axis=0, keepdims=True), axis=1, keepdims=True) + 1e-06
        scale = lax.rsqrt(square)
        done[p] = (raw * (CHI * CHI * scale)).astype(jnp.bfloat16)
        copy = pltpu.make_async_copy(done.at[p], coarse.at[p, row], sem.at[p])
        copy.start()
        copies.append(copy)
        diagonal = jnp.where(crossed, raw, 0.0)
        traced = jnp.sum(jnp.sum(diagonal, axis=0, keepdims=True), axis=1, keepdims=True)
        here = (small_row == row) & (small_col == p)
        all_logs = jnp.where(here, 0.5 * jnp.log(square), all_logs)
        all_traces = jnp.where(here, CHI * traced * scale, all_traces)
    logs[...] = all_logs
    traces[...] = all_traces
    for copy in copies:
        copy.wait()


def contract(row, halves, before):
    count = halves[0].shape[0] // 2
    anywhere = pl.BlockSpec(memory_space=pl.ANY)
    vmem = pl.BlockSpec(memory_space=pltpu.VMEM)
    small = jax.ShapeDtypeStruct if row else pltpu.VMEM
    before = before and (before[0],) + tuple(pltpu.with_memory_space_constraint(x, pltpu.VMEM) for x in before[1:])
    return pl.pallas_call(
        lambda *refs: contract_kernel(count, row, *refs),
        out_shape=(
            jax.ShapeDtypeStruct((count, 2, WIDE, WIDE), jnp.bfloat16),
            small((2, count), jnp.float32),
            small((2, count), jnp.float32),
        ),
        in_specs=[vmem] * len(halves) + [anywhere, vmem, vmem][: len(before)],
        out_specs=(anywhere, vmem, vmem),
        input_output_aliases={len(halves): 0} if before else {},
        scratch_shapes=[
            pltpu.VMEM((2, WIDE, WIDE), jnp.bfloat16),
            pltpu.VMEM((2, WIDE, WIDE), jnp.bfloat16),
            pltpu.VMEM((count, WIDE, WIDE), jnp.bfloat16),
            pltpu.SemaphoreType.DMA((count,)),
        ],
        name="contract",
    )(*[pltpu.with_memory_space_constraint(half, pltpu.VMEM) for half in halves], *before)


def pull(x, dx, dy):
    nx, ny = lax.axis_size("gx"), lax.axis_size("gy")
    pairs = [
        (i * ny + j, (i - dx) % nx * ny + (j - dy) % ny) for i in range(nx) for j in range(ny)
    ]
    return lax.ppermute(x, ("gx", "gy"), pairs)


def body(site_tensors, test_matrix):
    basis, second, above, right, corner = split_block(site_tensors, test_matrix)
    above = pull(above, 0, 1)
    right = pull(right, 1, 0)
    corner = pull(corner, 1, 1)
    before = contract(0, (basis, second), ())
    coarse, log_norm, trace = contract(1, (basis, above, right, corner), before)
    return coarse, log_norm.T, trace.T


def solution(mesh):
    in_specs = (P("gx", "gy", None, None), P("gx", "gy", None, None))
    out_specs = (P("gx", "gy", None, None), P("gx", "gy"), P("gx", "gy"))
    return jax.shard_map(body, mesh=mesh, in_specs=in_specs, out_specs=out_specs, check_vma=False)
```

time: 206 us -> 36.5 us (0.18)
  other arithmetic: 85.2 us -> 0 us
  local copies, waits for them, and re-layouts: 53.2 us -> 0 us
  matrix products: 17.5 us -> 0 us
  waiting for transfers between devices: 13.6 us -> 0.01 us
  Pallas kernels: 0 us -> 12.6 us
  starting transfers between devices: 34.2 us -> 23 us
    another operation x11 -> x0, other arithmetic: 80.4 us -> none  [the longest x4 43.2 us: split_block(): lower_factor = jnp.linalg.cholesky(gram_matrix)]
    convert_element_type x2 -> x0, local copies, waits for them, and re-layouts: 22.9 us -> none  [the longest x1 11.4 us: contract_sites(): pair_high = jnp.einsum('ncru,nevr->nceuv', high_left, high_right, preferr...]
    reshape x2 -> x0, local copies, waits for them, and re-layouts: 21.2 us -> none  [the longest x1 11.1 us: contract_sites(): pair_low = pair_low.reshape(count, width, width)]
    dot_general x6 -> x0, matrix products: 15.8 us -> none  [the longest x1 5.58 us: contract_sites(): jnp.einsum('naur,nbvr->nabuv', low_left, low_right, preferred_element_typ...]
    ppermute x4 -> x3, waiting for transfers between devices: 13.6 us -> 0.01 us  [pull(): return lax.ppermute(x, ('gx', 'gy'), pairs)]
    pallas_call x0 -> x3, Pallas kernels: none -> 12.6 us  [the longest x2 6.98 us: contract(): pl.pallas_call(lambda *refs: contract_kernel(count, row, *refs), out_shap...]
    ppermute x4 -> x3, starting transfers between devices: 34.2 us -> 23 us  [pull(): return lax.ppermute(x, ('gx', 'gy'), pairs)]
    unnamed x14 -> x0, local copies, waits for them, and re-layouts: 4 us -> none
  transfers between devices with their start and end apart: 4 -> 3, of which waited for: 2 -> 0; matrix products, arithmetic and copies ran while one was open for 2% -> 0% of each run, Pallas kernels for 0% -> 9%
where the time goes in v1:
time: 36.5 us; the launch traced here: 36.3 us
  starting transfers between devices  23 us (63%)
  Pallas kernels  12.6 us (35%)
  between operations  0.69 us (2%)
    ppermute x3, starting transfers between devices, pull(): return lax.ppermute(x, ('gx', 'gy'), pairs)  23 us
    pallas_call x2, Pallas kernels, contract(): pl.pallas_call(lambda *refs: contract_kernel(count, row, *refs), out_shap...  6.98 us
    pallas_call x1, Pallas kernels, split_block(): pl.pallas_call(lambda *refs: split_kernel(columns, rows, *refs), out_shap...  5.57 us
  transfers between devices with their start and end apart: 3, of which 0 were waited for; matrix products, arithmetic and copies ran while one was open for 0% of the time, Pallas kernels for 9%

profile of v1, /device:TPU:1, one launch (start us, length us, event | category | flops | bytes accessed | tf_op | source)
XLA Modules:
  0.0 36.3 jit_solution(6556654119418466321)
XLA Ops:
  0.6 5.6 %split.1 = (bf16[8,2,16,256]{3,2,1,0:T(8,128)(2,1)S(1)}, bf16[8,16,256]{2,1,0:T(8,128)(2,1)S(1)}, bf16[7,16,256]{2,1,0:T(8,128)(2,1)S(1)}, bf16[1,16,256]{2,1,0:T(8,128)(2,1)S(1)}, bf16[1,16,256]{2,1,0:T(8,128)(2,1)S(1)}) custom-call(bf16[8,2,256,256]{3,2,1,0:T(8,128)(2,1)} %refs_0_.1, bf16[8,2,16,256]{3,2,1,0:T(8,128)(2,1)} %refs_1_.1), custom_call_target="tpu_custom_call" | custom-call | tf_op jit(solution)/shard_map/split/pallas_call | solution.py:74
  6.2 14.4 %collective-permute-start = (bf16[7,16,256]{2,1,0:T(8,128)(2,1)S(1)}, bf16[7,16,256]{2,1,0:T(8,128)(2,1)S(1)}, u32[]{:S(2)}, u32[]{:S(2)}) collective-permute-start(bf16[7,16,256]{2,1,0:T(8,128)(2,1)S(1)} %get-tuple-element.15), channel_id=1, source_target_pairs={{0,31},{1,0},{2,1},{3,2},{4,3},{5,4},{6,5},{7,6},{8,7},{9,8},{10,9... | collective-permute-start | bytes 172040 | tf_op jit(solution)/shard_map/ppermute | solution.py:196
  20.6 2.9 %collective-permute-start.1 = (bf16[1,16,256]{2,1,0:T(8,128)(2,1)S(1)}, bf16[1,16,256]{2,1,0:T(8,128)(2,1)S(1)}, u32[]{:S(2)}, u32[]{:S(2)}) collective-permute-start(bf16[1,16,256]{2,1,0:T(8,128)(2,1)S(1)} %get-tuple-element.16), channel_id=1, source_target_pairs={{0,480},{1,481},{2,482},{3,483},{4,484},{5,485},{6,486},{7,487},{8... | collective-permute-start | bytes 24584 | tf_op jit(solution)/shard_map/ppermute | solution.py:196
  23.5 5.7 %collective-permute-start.2 = (bf16[1,16,256]{2,1,0:T(8,128)(2,1)S(1)}, bf16[1,16,256]{2,1,0:T(8,128)(2,1)S(1)}, u32[]{:S(2)}, u32[]{:S(2)}) collective-permute-start(bf16[1,16,256]{2,1,0:T(8,128)(2,1)S(1)} %get-tuple-element.17), channel_id=1, source_target_pairs={{0,511},{1,480},{2,481},{3,482},{4,483},{5,484},{6,485},{7,486},{8... | collective-permute-start | bytes 24584 | tf_op jit(solution)/shard_map/ppermute | solution.py:196
  29.2 3.2 %contract.2 = (bf16[4,2,256,256]{3,2,1,0:T(8,128)(2,1)}, f32[2,4]{1,0:T(2,128)S(1)}, f32[2,4]{1,0:T(2,128)S(1)}) custom-call(bf16[8,2,16,256]{3,2,1,0:T(8,128)(2,1)S(1)} %get-tuple-element.14.refs_0_, bf16[8,16,256]{2,1,0:T(8,128)(2,1)S(1)} %get-tuple-element.18.refs_1_), custom_call_target="tpu_custom_call" | custom-call | tf_op jit(solution)/shard_map/contract/pallas_call | solution.py:171
  32.5 0.0 collective-permute-done.1.refs_2_
  32.5 0.0 collective-permute-done.2.refs_3_
  32.5 0.0 collective-permute-done.refs_1_
  32.5 3.8 %contract.3 = (bf16[4,2,256,256]{3,2,1,0:T(8,128)(2,1)}, f32[2,4]{1,0:T(2,128)}, f32[2,4]{1,0:T(2,128)}) custom-call(bf16[8,2,16,256]{3,2,1,0:T(8,128)(2,1)S(1)} %get-tuple-element.14.refs_0_, bf16[7,16,256]{2,1,0:T(8,128)(2,1)S(1)} %collective-permute-done.refs_1_, ...), custom_call_target="tpu_custom_call", output_to_operand_aliasing={{0}: (4, {})} | custom-call | tf_op jit(solution)/shard_map/contract/pallas_call | solution.py:171
Async XLA Ops:
  6.2 26.3 %collective-permute-start = (bf16[7,16,256]{2,1,0:T(8,128)(2,1)S(1)}, bf16[7,16,256]{2,1,0:T(8,128)(2,1)S(1)}, u32[]{:S(2)}, u32[]{:S(2)}) collective-permute-start(bf16[7,16,256]{2,1,0:T(8,128)(2,1)S(1)} %get-tuple-element.15), channel_id=1, source_target_pairs={{0,31},{1,0},{2,1},{3,2},{4,3},{5,4},{6,5},{7,6},{8,7},{9,8},{10,9... | collective-permute-start | bytes 172040 | tf_op jit(solution)/shard_map/ppermute | solution.py:196
  20.6 11.8 %collective-permute-start.1 = (bf16[1,16,256]{2,1,0:T(8,128)(2,1)S(1)}, bf16[1,16,256]{2,1,0:T(8,128)(2,1)S(1)}, u32[]{:S(2)}, u32[]{:S(2)}) collective-permute-start(bf16[1,16,256]{2,1,0:T(8,128)(2,1)S(1)} %get-tuple-element.16), channel_id=1, source_target_pairs={{0,480},{1,481},{2,482},{3,483},{4,484},{5,485},{6,486},{7,487},{8... | collective-permute-start | bytes 24584 | tf_op jit(solution)/shard_map/ppermute | solution.py:196
  23.5 9.0 %collective-permute-start.2 = (bf16[1,16,256]{2,1,0:T(8,128)(2,1)S(1)}, bf16[1,16,256]{2,1,0:T(8,128)(2,1)S(1)}, u32[]{:S(2)}, u32[]{:S(2)}) collective-permute-start(bf16[1,16,256]{2,1,0:T(8,128)(2,1)S(1)} %get-tuple-element.17), channel_id=1, source_target_pairs={{0,511},{1,480},{2,481},{3,482},{4,483},{5,484},{6,485},{7,486},{8... | collective-permute-start | bytes 24584 | tf_op jit(solution)/shard_map/ppermute | solution.py:196

commit v2 on v1

v2 whole, which is shorter than its diff:
```python
import jax
import jax.numpy as jnp
from jax import lax
from jax.experimental import pallas as pl
from jax.experimental.pallas import tpu as pltpu
from jax.sharding import PartitionSpec as P

CHI = 16
WIDE = CHI * CHI
HALF = 128
NT = (((1,), (1,)), ((), ()))
NN = (((1,), (0,)), ((), ()))


ANY = pl.BlockSpec(memory_space=pl.ANY)
VMEM = pl.BlockSpec(memory_space=pltpu.VMEM)
GRANT = pltpu.CompilerParams(vmem_limit_bytes=32 << 20)


def near(*arrays):
    return [pltpu.with_memory_space_constraint(x, pltpu.VMEM) for x in arrays]


def dot(a, b, dims=NN):
    return lax.dot_general(a, b, dims, preferred_element_type=jnp.float32)


def split_sites(sources, slots, work):
    count = len(sources)
    for s, (test, tensor) in enumerate(sources):
        sketch = dot(test[...], tensor[...], NT)
        for slot in range(s, slots, count):
            for h in range(2):
                work[h, pl.ds(slot, CHI, stride=slots), :] = sketch[:, h * HALF : (h + 1) * HALF]

    def line(h, k):
        return work[h, k * slots : (k + 1) * slots, :]

    def inner(i, j):
        parts = line(0, i) * line(0, j) + line(1, i) * line(1, j)
        return jnp.broadcast_to(jnp.sum(parts, axis=1, keepdims=True), (slots, HALF))

    gram = {(i, j): inner(i, j) for j in range(CHI) for i in range(j, CHI)}
    for k in range(CHI):
        scale = lax.rsqrt(gram[k, k])
        lower = {i: gram[i, k] * scale for i in range(k + 1, CHI)}
        for i in range(k + 1, CHI):
            for j in range(k + 1, i + 1):
                gram[i, j] = gram[i, j] - lower[i] * lower[j]
        for h in range(2):
            row = line(h, k) * scale
            work[h, k * slots : (k + 1) * slots, :] = row
            for i in range(k + 1, CHI):
                work[h, i * slots : (i + 1) * slots, :] = line(h, i) - lower[i] * row
    for s, (_, tensor) in enumerate(sources):
        halves = [work[h, pl.ds(s, CHI, stride=slots), :] for h in range(2)]
        basis = jnp.concatenate(halves, axis=1).astype(jnp.bfloat16)
        yield s, basis, dot(basis, tensor[...]).astype(jnp.bfloat16)


def left_kernel(columns, rows, tensors, tests, leftmost, vm, vt, work, sem):
    copies = []
    for x in range(columns):
        copies.append(pltpu.make_async_copy(tests.at[x], vt.at[x], sem.at[0, x]))
        copies.append(pltpu.make_async_copy(tensors.at[x], vm.at[x], sem.at[1, x]))
    for copy in copies:
        copy.start()
    for copy in copies[:2]:
        copy.wait()
    for y, basis, second in split_sites([(vt.at[0, y], vm.at[0, y]) for y in range(rows)], 8, work):
        leftmost[1 - y] = basis if y == 1 else second
    for copy in copies[2:]:
        copy.wait()


def split_kernel(columns, rows, tensors, tests, basis, second, lowest, work):
    place = [(x, y) for x in range(columns) for y in range(rows)]
    for s, one, other in split_sites([(tests.at[x, y], tensors.at[x, y]) for x, y in place], len(place), work):
        x, y = place[s]
        basis[x, y] = one
        if y == 1:
            second[x] = other
        elif x > 0:
            lowest[x - 1] = other


def split_left(tensors, tests):
    columns, rows = tensors.shape[0], tensors.shape[1]
    return pl.pallas_call(
        lambda *refs: left_kernel(columns, rows, *refs),
        out_shape=[
            pltpu.VMEM((2, CHI, WIDE), jnp.bfloat16),
            pltpu.VMEM(tensors.shape, tensors.dtype),
            pltpu.VMEM(tests.shape, tests.dtype),
        ],
        in_specs=[ANY] * 2,
        out_specs=[VMEM] * 3,
        scratch_shapes=[pltpu.VMEM((2, CHI * 8, HALF), jnp.float32), pltpu.SemaphoreType.DMA((2, columns))],
        compiler_params=GRANT,
        name="split_left",
    )(*[pltpu.with_memory_space_constraint(x, pltpu.HBM) for x in (tensors, tests)])


def split_block(tensors, tests):
    columns, rows = tensors.shape[0], tensors.shape[1]
    shapes = [(columns, rows), (columns,), (columns,)]
    return pl.pallas_call(
        lambda *refs: split_kernel(columns, rows, *refs),
        out_shape=[pltpu.VMEM(shape + (CHI, WIDE), jnp.bfloat16) for shape in shapes],
        in_specs=[VMEM] * 2,
        out_specs=[VMEM] * 3,
        scratch_shapes=[pltpu.VMEM((2, CHI * columns * rows, HALF), jnp.float32)],
        compiler_params=GRANT,
        name="split",
    )(*near(tensors, tests))


def widen(half, pick, tile):
    spread = jnp.broadcast_to(half.astype(jnp.float32)[:, None, :], (CHI, CHI, WIDE)).reshape(WIDE, WIDE)
    spread = jnp.where(pick, spread, 0.0).astype(jnp.bfloat16)
    return dot(spread, tile).astype(jnp.bfloat16)


def pair_up(wide, other, own, out):
    left = jnp.concatenate([other[:, :HALF], other[:, HALF:]], axis=0)
    for a in range(0, CHI, 2):
        blocks = []
        for step in range(2):
            piece = wide[(a + step) * CHI : (a + step + 1) * CHI, :]
            zero = jnp.zeros_like(piece)
            blocks.append(jnp.concatenate([jnp.where(own[v], piece, zero) for v in range(8)], axis=0))
        got = dot(left, jnp.concatenate(blocks, axis=1)).astype(jnp.bfloat16)
        for step in range(2):
            base = (a + step) * CHI
            for h in range(2):
                out[base : base + CHI, h * HALF : (h + 1) * HALF] = got[
                    h * CHI : (h + 1) * CHI, step * HALF : (step + 1) * HALF
                ]


def patterns():
    iota = lambda shape, axis: lax.broadcasted_iota(jnp.int32, shape, axis)
    r, c = iota((WIDE, WIDE), 0), iota((WIDE, WIDE), 1)
    rt, ct = iota((WIDE, HALF), 0), iota((WIDE, HALF), 1)
    lane = iota((CHI, HALF), 1)
    return dict(
        pick_minor=(c % CHI) == (r % CHI),
        pick_major=(c // CHI) == (r % CHI),
        tile_major=((rt // CHI) == (ct % CHI)).astype(jnp.float32).astype(jnp.bfloat16),
        tile_minor=((rt % CHI) == (ct % CHI)).astype(jnp.float32).astype(jnp.bfloat16),
        own=[(lane // CHI) == v for v in range(8)],
        crossed=((c // CHI) == (r % CHI)) & ((c % CHI) == (r // CHI)),
        small=(iota((8, HALF), 0), iota((8, HALF), 1)),
    )


def contract_row(row, count, corners, coarse, stats, low, high, done, sem):
    at = patterns()
    rows, lanes = at["small"]
    copies = []
    for p in range(count):
        north_east, north_west, south_east, south_west = corners(p)
        pair_up(widen(north_east, at["pick_minor"], at["tile_major"]), north_west, at["own"], low.at[p % 2])
        pair_up(widen(south_east, at["pick_major"], at["tile_minor"]), south_west, at["own"], high.at[p % 2])
        raw = dot(low[p % 2], high[p % 2], NT)
        square = jnp.sum(jnp.sum(raw * raw, axis=0, keepdims=True), axis=1, keepdims=True) + 1e-06
        scale = lax.rsqrt(square)
        done[p] = (raw * (CHI * CHI * scale)).astype(jnp.bfloat16)
        copy = pltpu.make_async_copy(done.at[p], coarse.at[p, row], sem.at[p])
        copy.start()
        copies.append(copy)
        diagonal = jnp.where(at["crossed"], raw, 0.0)
        traced = jnp.sum(jnp.sum(diagonal, axis=0, keepdims=True), axis=1, keepdims=True)
        stats = jnp.where((rows == row) & (lanes == p), 0.5 * jnp.log(square), stats)
        stats = jnp.where((rows == 2 + row) & (lanes == p), CHI * traced * scale, stats)
    return stats, copies


def inner_kernel(count, kind, now, basis, second, *refs):
    stats_in = None
    if kind == "ahead":
        coarse, stats, low, high, done, sem = refs
    else:
        _, stats_in, coarse, stats, low, high, done, sem = refs

    def corners(p):
        return basis[2 * p, 0], basis[2 * p + 1, 0], second[2 * p], second[2 * p + 1]

    here = now()

    @pl.when(here)
    def _():
        got, copies = contract_row(0, count, corners, coarse, jnp.zeros((8, HALF), jnp.float32), low, high, done, sem)
        stats[...] = got
        for copy in copies:
            copy.wait()

    @pl.when(jnp.logical_not(here))
    def _():
        stats[...] = jnp.zeros((8, HALF), jnp.float32) if stats_in is None else stats_in[...]


def outer_kernel(count, now, alone, basis, above, leftmost, leftmost_alone, stats_in, *refs):
    coarse, logs, traces, lowest, low, high, done, sem, vs, sem_s = refs[-10:]
    apart = alone()
    right = jnp.where(jnp.full((CHI, WIDE), apart), leftmost_alone[0].astype(jnp.float32), leftmost[0].astype(jnp.float32))
    right = right.astype(jnp.bfloat16)

    @pl.when(apart)
    def _():
        lowest[2 * count - 1] = leftmost_alone[1]

    def corners(p):
        return basis[2 * p + 1, 1], basis[2 * p + 2, 1] if p < count - 1 else right, above[2 * p], above[2 * p + 1]

    @pl.when(now())
    def _():
        stats, copies = contract_row(1, count, corners, coarse, stats_in[...], low, high, done, sem)
        vs[0] = stats[0:2, :count]
        vs[1] = stats[2:4, :count]
        small = [pltpu.make_async_copy(vs.at[0], logs, sem_s.at[0]), pltpu.make_async_copy(vs.at[1], traces, sem_s.at[1])]
        for copy in small:
            copy.start()
        for copy in copies + small:
            copy.wait()


def scratch(count):
    return [
        pltpu.VMEM((2, WIDE, WIDE), jnp.bfloat16),
        pltpu.VMEM((2, WIDE, WIDE), jnp.bfloat16),
        pltpu.VMEM((count, WIDE, WIDE), jnp.bfloat16),
        pltpu.SemaphoreType.DMA((count,)),
    ]


def whole(count):
    return jax.ShapeDtypeStruct((count, 2, WIDE, WIDE), jnp.bfloat16)


def inner(kind, now, basis, second, *before):
    count = second.shape[0] // 2
    return pl.pallas_call(
        lambda *refs: inner_kernel(count, kind, now, *refs),
        out_shape=(whole(count), pltpu.VMEM((8, HALF), jnp.float32)),
        in_specs=[VMEM, VMEM, ANY, VMEM][: 2 + len(before)],
        out_specs=(ANY, VMEM),
        input_output_aliases={2: 0} if before else {},
        scratch_shapes=scratch(count),
        compiler_params=GRANT,
        name="inner_" + kind,
    )(*near(basis, second), *before[:1], *near(*before[1:]))


def pack(lowest, right, own, stats):
    def kernel(lowest_in, right_in, own_in, stats_in, lowest_out, own_out, stats_out):
        lowest_out[lowest.shape[0] - 1] = right_in[1]

    return pl.pallas_call(
        kernel,
        out_shape=[pltpu.VMEM(x.shape, x.dtype) for x in (lowest, own, stats)],
        in_specs=[VMEM] * 4,
        out_specs=[VMEM] * 3,
        input_output_aliases={0: 0, 2: 1, 3: 2},
        compiler_params=GRANT,
        name="pack",
    )(*near(lowest, right, own, stats))


def outer(now, alone, basis, above, leftmost, leftmost_alone, stats, lowest, coarse, *small):
    count = above.shape[0] // 2
    shape = jax.ShapeDtypeStruct((2, count), jnp.float32)
    return pl.pallas_call(
        lambda *refs: outer_kernel(count, now, alone, *refs),
        out_shape=(whole(count), shape, shape, pltpu.VMEM(lowest.shape, lowest.dtype)),
        in_specs=[VMEM] * 6 + [ANY] * (1 + len(small)),
        out_specs=(ANY, ANY, ANY, VMEM),
        input_output_aliases={5: 3, 6: 0} | {7 + k: 1 + k for k in range(len(small))},
        scratch_shapes=scratch(count) + [pltpu.VMEM((2, 2, count), jnp.float32), pltpu.SemaphoreType.DMA((2,))],
        compiler_params=GRANT,
        name="outer",
    )(*near(basis, above, leftmost, leftmost_alone, stats, lowest), coarse, *small)


def pull(x, dx, dy, takes):
    nx, ny = lax.axis_size("gx"), lax.axis_size("gy")
    pairs = [
        ((g + dx) % nx * ny + (h + dy) % ny, g * ny + h) for g in range(nx) for h in range(ny) if takes(g, h)
    ]
    return lax.ppermute(x, ("gx", "gy"), pairs)


def body(site_tensors, test_matrix):
    columns, rows = lax.axis_size("gx"), lax.axis_size("gy")
    half = 17 if rows > 17 else max(1, rows // 2)
    g = lambda: lax.axis_index("gx")
    h = lambda: lax.axis_index("gy")
    ahead = lambda: (h() == 0) & ((g() == 1) | (g() == columns - 1))
    near_rest = lambda: jnp.logical_not(ahead()) & (h() < half)
    alone = lambda: (g() == 0) & (h() == 0)
    leftmost, tensors, tests = split_left(site_tensors, test_matrix)
    right = pull(leftmost, 1, 0, lambda i, j: (i, j) != (0, 0))
    basis, second, lowest = split_block(tensors, tests)
    coarse, stats = inner("ahead", ahead, basis, second)
    lowest, leftmost, stats = pack(lowest, right, leftmost, stats)
    near_above = pull(lowest, 0, 1, lambda i, j: j < half)
    right_alone = pull(leftmost, 1, 0, lambda i, j: (i, j) == (0, 0))
    coarse, stats = inner("near", near_rest, basis, second, coarse, stats)
    coarse, log_norm, trace, lowest = outer(
        lambda: h() < half, alone, basis, near_above, right, right_alone, stats, lowest, coarse
    )
    far_above = pull(lowest, 0, 1, lambda i, j: j >= half)
    coarse, stats = inner("far", lambda: h() >= half, basis, second, coarse, stats)
    coarse, log_norm, trace, _ = outer(
        lambda: h() >= half, alone, basis, far_above, right, right_alone, stats, lowest, coarse, log_norm, trace
    )
    return coarse, log_norm.T, trace.T


def solution(mesh):
    in_specs = (P("gx", "gy", None, None), P("gx", "gy", None, None))
    out_specs = (P("gx", "gy", None, None), P("gx", "gy"), P("gx", "gy"))
    return jax.shard_map(body, mesh=mesh, in_specs=in_specs, out_specs=out_specs, check_vma=False)
```

time: 36.5 us -> 25.8 us (0.71)
  the two profiles are of different devices: /device:TPU:1 before, /device:TPU:288 now
where the time goes in v2:
time: 25.8 us; the launch traced here: 25.5 us
  starting transfers between devices  14.8 us (57%)
  Pallas kernels  9.89 us (38%)
  between operations  0.74 us (3%)
    ppermute x4, starting transfers between devices, pull(): return lax.ppermute(x, ('gx', 'gy'), pairs)  14.8 us
    pallas_call x3, Pallas kernels, inner(): pl.pallas_call(lambda *refs: inner_kernel(count, kind, now, *refs), out_s...  3.32 us
    pallas_call x2, Pallas kernels, outer(): pl.pallas_call(lambda *refs: outer_kernel(count, now, alone, *refs), out_...  3.32 us
    pallas_call x1, Pallas kernels, split_left(): pl.pallas_call(lambda *refs: left_kernel(columns, rows, *refs), out_shape...  1.84 us
    pallas_call x1, Pallas kernels, split_block(): pl.pallas_call(lambda *refs: split_kernel(columns, rows, *refs), out_shap...  1.41 us
  transfers between devices with their start and end apart: 4, of which 0 were waited for; matrix products, arithmetic and copies ran while one was open for 0% of the time, Pallas kernels for 19%

profile of v2, /device:TPU:288, one launch (start us, length us, event | category | flops | bytes accessed | tf_op | source)
XLA Modules:
  0.0 25.5 jit_solution(7802919994021128972)
XLA Ops:
  0.6 1.8 %split_left.1 = (bf16[2,16,256]{2,1,0:T(8,128)(2,1)S(1)}, bf16[8,2,256,256]{3,2,1,0:T(8,128)(2,1)S(1)}, bf16[8,2,16,256]{3,2,1,0:T(8,128)(2,1)S(1)}) custom-call(bf16[8,2,256,256]{3,2,1,0:T(8,128)(2,1)} %refs_0_.1, bf16[8,2,16,256]{3,2,1,0:T(8,128)(2,1)} %refs_1_.1), custom_call_target="tpu_custom_call" | custom-call | tf_op jit(solution)/shard_map/split_left/pallas_call | solution.py:89
  2.5 5.3 %collective-permute-start = (bf16[2,16,256]{2,1,0:T(8,128)(2,1)S(1)}, bf16[2,16,256]{2,1,0:T(8,128)(2,1)S(1)}, u32[]{:S(2)}, u32[]{:S(2)}) collective-permute-start(bf16[2,16,256]{2,1,0:T(8,128)(2,1)S(1)} %get-tuple-element.29.own_in), channel_id=1, source_target_pairs={{33,1},{34,2},{35,3},{36,4},{37,5},{38,6},{39,7},{40,8},{41,9},{42... | collective-permute-start | bytes 49160 | tf_op jit(solution)/shard_map/ppermute | solution.py:290
  7.8 1.4 %split.1 = (bf16[8,2,16,256]{3,2,1,0:T(8,128)(2,1)S(1)}, bf16[8,16,256]{2,1,0:T(8,128)(2,1)S(1)}, bf16[8,16,256]{2,1,0:T(8,128)(2,1)S(1)}) custom-call(bf16[8,2,256,256]{3,2,1,0:T(8,128)(2,1)S(1)} %get-tuple-element.25.refs_0_, bf16[8,2,16,256]{3,2,1,0:T(8,128)(2,1)S(1)} %get-tuple-element.26.refs_1_), custom_call_target="tpu_custom_call" | custom-call | tf_op jit(solution)/shard_map/split/pallas_call | solution.py:107
  9.2 0.1 inner_ahead.1
  9.2 0.0 collective-permute-done.right_in.refs_2_
  9.3 0.7 %collective-permute-start.1 = (bf16[8,16,256]{2,1,0:T(8,128)(2,1)S(1)}, bf16[8,16,256]{2,1,0:T(8,128)(2,1)S(1)}, u32[]{:S(2)}, u32[]{:S(2)}) collective-permute-start(bf16[8,16,256]{2,1,0:T(8,128)(2,1)S(1)} %get-tuple-element.32.refs_5_), channel_id=1, source_target_pairs={{1,0},{2,1},{3,2},{4,3},{5,4},{6,5},{7,6},{8,7},{9,8},{10,9},{11,1... | collective-permute-start | bytes 196616 | tf_op jit(solution)/shard_map/ppermute | solution.py:290
  9.9 0.7 %collective-permute-start.2 = (bf16[2,16,256]{2,1,0:T(8,128)(2,1)S(1)}, bf16[2,16,256]{2,1,0:T(8,128)(2,1)S(1)}, u32[]{:S(2)}, u32[]{:S(2)}) collective-permute-start(bf16[2,16,256]{2,1,0:T(8,128)(2,1)S(1)} %get-tuple-element.33), channel_id=1, source_target_pairs={{32,0}} | collective-permute-start | bytes 49160 | tf_op jit(solution)/shard_map/ppermute | solution.py:290
  10.6 0.1 inner_near.1
  10.7 0.0 collective-permute-done.2.refs_3_
  10.7 0.0 collective-permute-done.1.refs_1_
  10.7 0.1 outer.2
  10.8 8.2 %collective-permute-start.3 = (bf16[8,16,256]{2,1,0:T(8,128)(2,1)S(1)}, bf16[8,16,256]{2,1,0:T(8,128)(2,1)S(1)}, u32[]{:S(2)}, u32[]{:S(2)}) collective-permute-start(bf16[8,16,256]{2,1,0:T(8,128)(2,1)S(1)} %get-tuple-element.38.refs_5_), channel_id=1, source_target_pairs={{18,17},{19,18},{20,19},{21,20},{22,21},{23,22},{24,23},{25,24},{2... | collective-permute-start | bytes 196616 | tf_op jit(solution)/shard_map/ppermute | solution.py:290
  19.0 3.2 %inner_far.1 = (bf16[4,2,256,256]{3,2,1,0:T(8,128)(2,1)}, f32[8,128]{1,0:T(8,128)S(1)}) custom-call(bf16[8,2,16,256]{3,2,1,0:T(8,128)(2,1)S(1)} %get-tuple-element.27.refs_0_, bf16[8,16,256]{2,1,0:T(8,128)(2,1)S(1)} %get-tuple-element.30.refs_1_, bf16[4,2,256,256]{3,2,1,0:T(8,128)(2,1)} %get-tuple-element.39.refs_2_, ...), custom_call_target="tpu_custom_call", output_to_operand_aliasing={{0}: (2, {})} | custom-call | tf_op jit(solution)/shard_map/inner_far/pallas_call | solution.py:243
  22.2 0.0 collective-permute-done.3.refs_1_
  22.2 3.2 %outer.3 = (bf16[4,2,256,256]{3,2,1,0:T(8,128)(2,1)}, f32[2,4]{1,0:T(2,128)}, f32[2,4]{1,0:T(2,128)}, bf16[8,16,256]{2,1,0:T(8,128)(2,1)S(1)}) custom-call(bf16[8,2,16,256]{3,2,1,0:T(8,128)(2,1)S(1)} %get-tuple-element.27.refs_0_, ...), custom_call_target="tpu_custom_call", output_to_operand_aliasing={{3}: (5, {}), {0}: (6, {}), {1}: (7, {}), {2}: (8, {})} | custom-call | tf_op jit(solution)/shard_map/outer/pallas_call | solution.py:273
  (1 shorter events, 0.0 us)
Async XLA Ops:
  2.5 6.8 %collective-permute-start = (bf16[2,16,256]{2,1,0:T(8,128)(2,1)S(1)}, bf16[2,16,256]{2,1,0:T(8,128)(2,1)S(1)}, u32[]{:S(2)}, u32[]{:S(2)}) collective-permute-start(bf16[2,16,256]{2,1,0:T(8,128)(2,1)S(1)} %get-tuple-element.29.own_in), channel_id=1, source_target_pairs={{33,1},{34,2},{35,3},{36,4},{37,5},{38,6},{39,7},{40,8},{41,9},{42... | collective-permute-start | bytes 49160 | tf_op jit(solution)/shard_map/ppermute | solution.py:290
  9.3 1.4 %collective-permute-start.1 = (bf16[8,16,256]{2,1,0:T(8,128)(2,1)S(1)}, bf16[8,16,256]{2,1,0:T(8,128)(2,1)S(1)}, u32[]{:S(2)}, u32[]{:S(2)}) collective-permute-start(bf16[8,16,256]{2,1,0:T(8,128)(2,1)S(1)} %get-tuple-element.32.refs_5_), channel_id=1, source_target_pairs={{1,0},{2,1},{3,2},{4,3},{5,4},{6,5},{7,6},{8,7},{9,8},{10,9},{11,1... | collective-permute-start | bytes 196616 | tf_op jit(solution)/shard_map/ppermute | solution.py:290
  9.9 0.7 %collective-permute-start.2 = (bf16[2,16,256]{2,1,0:T(8,128)(2,1)S(1)}, bf16[2,16,256]{2,1,0:T(8,128)(2,1)S(1)}, u32[]{:S(2)}, u32[]{:S(2)}) collective-permute-start(bf16[2,16,256]{2,1,0:T(8,128)(2,1)S(1)} %get-tuple-element.33), channel_id=1, source_target_pairs={{32,0}} | collective-permute-start | bytes 49160 | tf_op jit(solution)/shard_map/ppermute | solution.py:290
  10.8 11.5 %collective-permute-start.3 = (bf16[8,16,256]{2,1,0:T(8,128)(2,1)S(1)}, bf16[8,16,256]{2,1,0:T(8,128)(2,1)S(1)}, u32[]{:S(2)}, u32[]{:S(2)}) collective-permute-start(bf16[8,16,256]{2,1,0:T(8,128)(2,1)S(1)} %get-tuple-element.38.refs_5_), channel_id=1, source_target_pairs={{18,17},{19,18},{20,19},{21,20},{22,21},{23,22},{24,23},{25,24},{2... | collective-permute-start | bytes 196616 | tf_op jit(solution)/shard_map/ppermute | solution.py:290

commit v3 on v2

--- a/solution.py
+++ b/solution.py
@@ -158,11 +158,15 @@
     at = patterns()
     rows, lanes = at["small"]
     copies = []
+    pairs = []
     for p in range(count):
         north_east, north_west, south_east, south_west = corners(p)
-        pair_up(widen(north_east, at["pick_minor"], at["tile_major"]), north_west, at["own"], low.at[p % 2])
-        pair_up(widen(south_east, at["pick_major"], at["tile_minor"]), south_west, at["own"], high.at[p % 2])
-        raw = dot(low[p % 2], high[p % 2], NT)
+        pairs.append((widen(north_east, at["pick_minor"], at["tile_major"]), north_west, low.at[p]))
+        pairs.append((widen(south_east, at["pick_major"], at["tile_minor"]), south_west, high.at[p]))
+    for wide, other, out in pairs:
+        pair_up(wide, other, at["own"], out)
+    products = [dot(low[p], high[p], NT) for p in range(count)]
+    for p, raw in enumerate(products):
         square = jnp.sum(jnp.sum(raw * raw, axis=0, keepdims=True), axis=1, keepdims=True) + 1e-06
         scale = lax.rsqrt(square)
         done[p] = (raw * (CHI * CHI * scale)).astype(jnp.bfloat16)
@@ -200,18 +204,12 @@
         stats[...] = jnp.zeros((8, HALF), jnp.float32) if stats_in is None else stats_in[...]
 
 
-def outer_kernel(count, now, alone, basis, above, leftmost, leftmost_alone, stats_in, *refs):
-    coarse, logs, traces, lowest, low, high, done, sem, vs, sem_s = refs[-10:]
-    apart = alone()
-    right = jnp.where(jnp.full((CHI, WIDE), apart), leftmost_alone[0].astype(jnp.float32), leftmost[0].astype(jnp.float32))
-    right = right.astype(jnp.bfloat16)
-
-    @pl.when(apart)
-    def _():
-        lowest[2 * count - 1] = leftmost_alone[1]
+def outer_kernel(count, now, basis, above, right, stats_in, *refs):
+    coarse, logs, traces, _, low, high, done, sem, vs, sem_s = refs[-10:]
 
     def corners(p):
-        return basis[2 * p + 1, 1], basis[2 * p + 2, 1] if p < count - 1 else right, above[2 * p], above[2 * p + 1]
+        beside = basis[2 * p + 2, 1] if p < count - 1 else right[0]
+        return basis[2 * p + 1, 1], beside, above[2 * p], above[2 * p + 1]
 
     @pl.when(now())
     def _():
@@ -227,8 +225,8 @@
 
 def scratch(count):
     return [
-        pltpu.VMEM((2, WIDE, WIDE), jnp.bfloat16),
-        pltpu.VMEM((2, WIDE, WIDE), jnp.bfloat16),
+        pltpu.VMEM((count, WIDE, WIDE), jnp.bfloat16),
+        pltpu.VMEM((count, WIDE, WIDE), jnp.bfloat16),
         pltpu.VMEM((count, WIDE, WIDE), jnp.bfloat16),
         pltpu.SemaphoreType.DMA((count,)),
     ]
@@ -252,41 +250,39 @@
     )(*near(basis, second), *before[:1], *near(*before[1:]))
 
 
-def pack(lowest, right, own, stats):
-    def kernel(lowest_in, right_in, own_in, stats_in, lowest_out, own_out, stats_out):
+def pack(lowest, right, stats):
+    def kernel(lowest_in, right_in, stats_in, lowest_out, stats_out):
         lowest_out[lowest.shape[0] - 1] = right_in[1]
 
     return pl.pallas_call(
         kernel,
-        out_shape=[pltpu.VMEM(x.shape, x.dtype) for x in (lowest, own, stats)],
-        in_specs=[VMEM] * 4,
-        out_specs=[VMEM] * 3,
-        input_output_aliases={0: 0, 2: 1, 3: 2},
+        out_shape=[pltpu.VMEM(x.shape, x.dtype) for x in (lowest, stats)],
+        in_specs=[VMEM] * 3,
+        out_specs=[VMEM] * 2,
+        input_output_aliases={0: 0, 2: 1},
         compiler_params=GRANT,
         name="pack",
-    )(*near(lowest, right, own, stats))
-
-
-def outer(now, alone, basis, above, leftmost, leftmost_alone, stats, lowest, coarse, *small):
+    )(*near(lowest, right, stats))
+
+
+def outer(now, basis, above, right, stats, lowest, coarse, *small):
     count = above.shape[0] // 2
     shape = jax.ShapeDtypeStruct((2, count), jnp.float32)
     return pl.pallas_call(
-        lambda *refs: outer_kernel(count, now, alone, *refs),
+        lambda *refs: outer_kernel(count, now, *refs),
         out_shape=(whole(count), shape, shape, pltpu.VMEM(lowest.shape, lowest.dtype)),
-        in_specs=[VMEM] * 6 + [ANY] * (1 + len(small)),
+        in_specs=[VMEM] * 5 + [ANY] * (1 + len(small)),
         out_specs=(ANY, ANY, ANY, VMEM),
-        input_output_aliases={5: 3, 6: 0} | {7 + k: 1 + k for k in range(len(small))},
+        input_output_aliases={4: 3, 5: 0} | {6 + k: 1 + k for k in range(len(small))},
         scratch_shapes=scratch(count) + [pltpu.VMEM((2, 2, count), jnp.float32), pltpu.SemaphoreType.DMA((2,))],
         compiler_params=GRANT,
         name="outer",
-    )(*near(basis, above, leftmost, leftmost_alone, stats, lowest), coarse, *small)
-
-
-def pull(x, dx, dy, takes):
+    )(*near(basis, above, right, stats, lowest), coarse, *small)
+
+
+def pull(x, dx, dy, takes=lambda h: True):
     nx, ny = lax.axis_size("gx"), lax.axis_size("gy")
-    pairs = [
-        ((g + dx) % nx * ny + (h + dy) % ny, g * ny + h) for g in range(nx) for h in range(ny) if takes(g, h)
-    ]
+    pairs = [((g + dx) % nx * ny + (h + dy) % ny, g * ny + h) for g in range(nx) for h in range(ny) if takes(h)]
     return lax.ppermute(x, ("gx", "gy"), pairs)
 
 
@@ -295,24 +291,19 @@
     half = 17 if rows > 17 else max(1, rows // 2)
     g = lambda: lax.axis_index("gx")
     h = lambda: lax.axis_index("gy")
-    ahead = lambda: (h() == 0) & ((g() == 1) | (g() == columns - 1))
-    near_rest = lambda: jnp.logical_not(ahead()) & (h() < half)
-    alone = lambda: (g() == 0) & (h() == 0)
+    ahead = lambda: (h() == 0) & (g() == columns - 1)
     leftmost, tensors, tests = split_left(site_tensors, test_matrix)
-    right = pull(leftmost, 1, 0, lambda i, j: (i, j) != (0, 0))
+    right = pull(leftmost, 1, 0)
     basis, second, lowest = split_block(tensors, tests)
     coarse, stats = inner("ahead", ahead, basis, second)
-    lowest, leftmost, stats = pack(lowest, right, leftmost, stats)
-    near_above = pull(lowest, 0, 1, lambda i, j: j < half)
-    right_alone = pull(leftmost, 1, 0, lambda i, j: (i, j) == (0, 0))
-    coarse, stats = inner("near", near_rest, basis, second, coarse, stats)
-    coarse, log_norm, trace, lowest = outer(
-        lambda: h() < half, alone, basis, near_above, right, right_alone, stats, lowest, coarse
-    )
-    far_above = pull(lowest, 0, 1, lambda i, j: j >= half)
+    lowest, stats = pack(lowest, right, stats)
+    near_above = pull(lowest, 0, 1, lambda h: h < half)
+    coarse, stats = inner("near", lambda: jnp.logical_not(ahead()) & (h() < half), basis, second, coarse, stats)
+    coarse, log_norm, trace, lowest = outer(lambda: h() < half, basis, near_above, right, stats, lowest, coarse)
+    far_above = pull(lowest, 0, 1, lambda h: h >= half)
     coarse, stats = inner("far", lambda: h() >= half, basis, second, coarse, stats)
     coarse, log_norm, trace, _ = outer(
-        lambda: h() >= half, alone, basis, far_above, right, right_alone, stats, lowest, coarse, log_norm, trace
+        lambda: h() >= half, basis, far_above, right, stats, lowest, coarse, log_norm, trace
     )
     return coarse, log_norm.T, trace.T
 

time: 25.8 us -> 24.9 us (0.965)
  the two profiles are of different devices: /device:TPU:288 before, /device:TPU:1 now
where the time goes in v3:
time: 24.9 us; the launch traced here: 24.7 us
  starting transfers between devices  11.4 us (46%)
  Pallas kernels  7.64 us (31%)
  waiting for transfers between devices  4.94 us (20%)
  between operations  0.71 us (3%)
    ppermute x3, starting transfers between devices, pull(): return lax.ppermute(x, ('gx', 'gy'), pairs)  11.4 us
    ppermute x3, waiting for transfers between devices, pull(): return lax.ppermute(x, ('gx', 'gy'), pairs)  4.94 us
    pallas_call x3, Pallas kernels, inner(): pl.pallas_call(lambda *refs: inner_kernel(count, kind, now, *refs), out_s...  2.22 us
    pallas_call x2, Pallas kernels, outer(): pl.pallas_call(lambda *refs: outer_kernel(count, now, *refs), out_shape=(...  2.17 us
    pallas_call x1, Pallas kernels, split_left(): pl.pallas_call(lambda *refs: left_kernel(columns, rows, *refs), out_shape...  1.84 us
    pallas_call x1, Pallas kernels, split_block(): pl.pallas_call(lambda *refs: split_kernel(columns, rows, *refs), out_shap...  1.41 us
  transfers between devices with their start and end apart: 3, of which 2 were waited for; matrix products, arithmetic and copies ran while one was open for 0% of the time, Pallas kernels for 15%

profile of v3, /device:TPU:1, one launch (start us, length us, event | category | flops | bytes accessed | tf_op | source)
XLA Modules:
  0.0 24.7 jit_solution(3771669543199805305)
XLA Ops:
  0.6 1.8 %split_left.1 = (bf16[2,16,256]{2,1,0:T(8,128)(2,1)S(1)}, bf16[8,2,256,256]{3,2,1,0:T(8,128)(2,1)S(1)}, bf16[8,2,16,256]{3,2,1,0:T(8,128)(2,1)S(1)}) custom-call(bf16[8,2,256,256]{3,2,1,0:T(8,128)(2,1)} %refs_0_.1, bf16[8,2,16,256]{3,2,1,0:T(8,128)(2,1)} %refs_1_.1), custom_call_target="tpu_custom_call" | custom-call | tf_op jit(solution)/shard_map/split_left/pallas_call | solution.py:89
  2.5 8.8 %collective-permute-start = (bf16[2,16,256]{2,1,0:T(8,128)(2,1)S(1)}, bf16[2,16,256]{2,1,0:T(8,128)(2,1)S(1)}, u32[]{:S(2)}, u32[]{:S(2)}) collective-permute-start(bf16[2,16,256]{2,1,0:T(8,128)(2,1)S(1)} %get-tuple-element.28), channel_id=1, source_target_pairs={{32,0},{33,1},{34,2},{35,3},{36,4},{37,5},{38,6},{39,7},{40,8},{41... | collective-permute-start | bytes 49160 | tf_op jit(solution)/shard_map/ppermute | solution.py:286
  11.3 1.4 %split.1 = (bf16[8,2,16,256]{3,2,1,0:T(8,128)(2,1)S(1)}, bf16[8,16,256]{2,1,0:T(8,128)(2,1)S(1)}, bf16[8,16,256]{2,1,0:T(8,128)(2,1)S(1)}) custom-call(bf16[8,2,256,256]{3,2,1,0:T(8,128)(2,1)S(1)} %get-tuple-element.24.refs_0_, bf16[8,2,16,256]{3,2,1,0:T(8,128)(2,1)S(1)} %get-tuple-element.25.refs_1_), custom_call_target="tpu_custom_call" | custom-call | tf_op jit(solution)/shard_map/split/pallas_call | solution.py:107
  12.7 0.1 inner_ahead.1
  12.7 0.0 collective-permute-done.right_in.refs_2_
  12.8 1.3 %collective-permute-start.1 = (bf16[8,16,256]{2,1,0:T(8,128)(2,1)S(1)}, bf16[8,16,256]{2,1,0:T(8,128)(2,1)S(1)}, u32[]{:S(2)}, u32[]{:S(2)}) collective-permute-start(bf16[8,16,256]{2,1,0:T(8,128)(2,1)S(1)} %get-tuple-element.31.refs_4_), channel_id=1, source_target_pairs={{1,0},{2,1},{3,2},{4,3},{5,4},{6,5},{7,6},{8,7},{9,8},{10,9},{11,1... | collective-permute-start | bytes 196616 | tf_op jit(solution)/shard_map/ppermute | solution.py:286
  14.1 2.1 %inner_near.1 = (bf16[4,2,256,256]{3,2,1,0:T(8,128)(2,1)}, f32[8,128]{1,0:T(8,128)S(1)}) custom-call(bf16[8,2,16,256]{3,2,1,0:T(8,128)(2,1)S(1)} %get-tuple-element.26.refs_0_, bf16[8,16,256]{2,1,0:T(8,128)(2,1)S(1)} %get-tuple-element.29.refs_1_, bf16[4,2,256,256]{3,2,1,0:T(8,128)(2,1)} %get-tuple-element.32.refs_2_, ...), custom_call_target="tpu_custom_call", output_to_operand_aliasing={{0}: (2, {})} | custom-call | tf_op jit(solution)/shard_map/inner_near/pallas_call | solution.py:241
  16.2 3.7 %collective-permute-done.1.refs_1_ = bf16[8,16,256]{2,1,0:T(8,128)(2,1)S(1)} collective-permute-done((bf16[8,16,256]{2,1,0:T(8,128)(2,1)S(1)}, bf16[8,16,256]{2,1,0:T(8,128)(2,1)S(1)}, u32[]{:S(2)}, u32[]{:S(2)}) %collective-permute-start.1) | collective-permute-done | bytes 65568 | tf_op jit(solution)/shard_map/ppermute | solution.py:286
  19.9 2.1 %outer.2 = (bf16[4,2,256,256]{3,2,1,0:T(8,128)(2,1)}, f32[2,4]{1,0:T(2,128)}, f32[2,4]{1,0:T(2,128)}, bf16[8,16,256]{2,1,0:T(8,128)(2,1)S(1)}) custom-call(bf16[8,2,16,256]{3,2,1,0:T(8,128)(2,1)S(1)} %get-tuple-element.26.refs_0_, bf16[8,16,256]{2,1,0:T(8,128)(2,1)S(1)} %collective-permute-done.1.refs_1_, ...), custom_call_target="tpu_custom_call", output_to_operand_aliasing={{3}: (4, {}), {0}: (5, {})} | custom-call | tf_op jit(solution)/shard_map/outer/pallas_call | solution.py:271
  22.0 1.3 %collective-permute-start.2 = (bf16[8,16,256]{2,1,0:T(8,128)(2,1)S(1)}, bf16[8,16,256]{2,1,0:T(8,128)(2,1)S(1)}, u32[]{:S(2)}, u32[]{:S(2)}) collective-permute-start(bf16[8,16,256]{2,1,0:T(8,128)(2,1)S(1)} %get-tuple-element.36.refs_4_), channel_id=1, source_target_pairs={{18,17},{19,18},{20,19},{21,20},{22,21},{23,22},{24,23},{25,24},{2... | collective-permute-start | bytes 196616 | tf_op jit(solution)/shard_map/ppermute | solution.py:286
  23.3 0.1 inner_far.1
  23.4 1.2 %collective-permute-done.2.refs_1_ = bf16[8,16,256]{2,1,0:T(8,128)(2,1)S(1)} collective-permute-done((bf16[8,16,256]{2,1,0:T(8,128)(2,1)S(1)}, bf16[8,16,256]{2,1,0:T(8,128)(2,1)S(1)}, u32[]{:S(2)}, u32[]{:S(2)}) %collective-permute-start.2) | collective-permute-done | bytes 65568 | tf_op jit(solution)/shard_map/ppermute | solution.py:286
  24.6 0.1 outer.3
  (1 shorter events, 0.0 us)
Async XLA Ops:
  2.5 10.3 %collective-permute-start = (bf16[2,16,256]{2,1,0:T(8,128)(2,1)S(1)}, bf16[2,16,256]{2,1,0:T(8,128)(2,1)S(1)}, u32[]{:S(2)}, u32[]{:S(2)}) collective-permute-start(bf16[2,16,256]{2,1,0:T(8,128)(2,1)S(1)} %get-tuple-element.28), channel_id=1, source_target_pairs={{32,0},{33,1},{34,2},{35,3},{36,4},{37,5},{38,6},{39,7},{40,8},{41... | collective-permute-start | bytes 49160 | tf_op jit(solution)/shard_map/ppermute | solution.py:286
  12.8 7.1 %collective-permute-start.1 = (bf16[8,16,256]{2,1,0:T(8,128)(2,1)S(1)}, bf16[8,16,256]{2,1,0:T(8,128)(2,1)S(1)}, u32[]{:S(2)}, u32[]{:S(2)}) collective-permute-start(bf16[8,16,256]{2,1,0:T(8,128)(2,1)S(1)} %get-tuple-element.31.refs_4_), channel_id=1, source_target_pairs={{1,0},{2,1},{3,2},{4,3},{5,4},{6,5},{7,6},{8,7},{9,8},{10,9},{11,1... | collective-permute-start | bytes 196616 | tf_op jit(solution)/shard_map/ppermute | solution.py:286
  22.0 2.6 %collective-permute-start.2 = (bf16[8,16,256]{2,1,0:T(8,128)(2,1)S(1)}, bf16[8,16,256]{2,1,0:T(8,128)(2,1)S(1)}, u32[]{:S(2)}, u32[]{:S(2)}) collective-permute-start(bf16[8,16,256]{2,1,0:T(8,128)(2,1)S(1)} %get-tuple-element.36.refs_4_), channel_id=1, source_target_pairs={{18,17},{19,18},{20,19},{21,20},{22,21},{23,22},{24,23},{25,24},{2... | collective-permute-start | bytes 196616 | tf_op jit(solution)/shard_map/ppermute | solution.py:286

commit v4 on v3

--- a/solution.py
+++ b/solution.py
@@ -60,9 +60,9 @@
 
 def left_kernel(columns, rows, tensors, tests, leftmost, vm, vt, work, sem):
     copies = []
-    for x in range(columns):
-        copies.append(pltpu.make_async_copy(tests.at[x], vt.at[x], sem.at[0, x]))
-        copies.append(pltpu.make_async_copy(tensors.at[x], vm.at[x], sem.at[1, x]))
+    for k, part in enumerate((pl.ds(0, 1), pl.ds(1, columns - 1))):
+        copies.append(pltpu.make_async_copy(tests.at[part], vt.at[part], sem.at[0, k]))
+        copies.append(pltpu.make_async_copy(tensors.at[part], vm.at[part], sem.at[1, k]))
     for copy in copies:
         copy.start()
     for copy in copies[:2]:
@@ -95,7 +95,7 @@
         ],
         in_specs=[ANY] * 2,
         out_specs=[VMEM] * 3,
-        scratch_shapes=[pltpu.VMEM((2, CHI * 8, HALF), jnp.float32), pltpu.SemaphoreType.DMA((2, columns))],
+        scratch_shapes=[pltpu.VMEM((2, CHI * 8, HALF), jnp.float32), pltpu.SemaphoreType.DMA((2, 2))],
         compiler_params=GRANT,
         name="split_left",
     )(*[pltpu.with_memory_space_constraint(x, pltpu.HBM) for x in (tensors, tests)])

time: 24.9 us -> 24.8 us (level)
  no operation moved by 1% of the time
where the time goes in v4:
time: 24.8 us; the launch traced here: 24.5 us
  starting transfers between devices  11.4 us (46%)
  Pallas kernels  7.51 us (30%)
  waiting for transfers between devices  4.95 us (20%)
  between operations  0.71 us (3%)
    ppermute x3, starting transfers between devices, pull(): return lax.ppermute(x, ('gx', 'gy'), pairs)  11.4 us
    ppermute x3, waiting for transfers between devices, pull(): return lax.ppermute(x, ('gx', 'gy'), pairs)  4.95 us
    pallas_call x3, Pallas kernels, inner(): pl.pallas_call(lambda *refs: inner_kernel(count, kind, now, *refs), out_s...  2.21 us
    pallas_call x2, Pallas kernels, outer(): pl.pallas_call(lambda *refs: outer_kernel(count, now, *refs), out_shape=(...  2.17 us
    pallas_call x1, Pallas kernels, split_left(): pl.pallas_call(lambda *refs: left_kernel(columns, rows, *refs), out_shape...  1.71 us
    pallas_call x1, Pallas kernels, split_block(): pl.pallas_call(lambda *refs: split_kernel(columns, rows, *refs), out_shap...  1.41 us
  transfers between devices with their start and end apart: 3, of which 2 were waited for; matrix products, arithmetic and copies ran while one was open for 0% of the time, Pallas kernels for 15%

profile of v4, /device:TPU:1, one launch (start us, length us, event | category | flops | bytes accessed | tf_op | source)
XLA Modules:
  0.0 24.5 jit_solution(244392955842023112)
XLA Ops:
  0.6 1.7 %split_left.1 = (bf16[2,16,256]{2,1,0:T(8,128)(2,1)S(1)}, bf16[8,2,256,256]{3,2,1,0:T(8,128)(2,1)S(1)}, bf16[8,2,16,256]{3,2,1,0:T(8,128)(2,1)S(1)}) custom-call(bf16[8,2,256,256]{3,2,1,0:T(8,128)(2,1)} %refs_0_.1, bf16[8,2,16,256]{3,2,1,0:T(8,128)(2,1)} %refs_1_.1), custom_call_target="tpu_custom_call" | custom-call | tf_op jit(solution)/shard_map/split_left/pallas_call | solution.py:89
  2.4 8.8 %collective-permute-start = (bf16[2,16,256]{2,1,0:T(8,128)(2,1)S(1)}, bf16[2,16,256]{2,1,0:T(8,128)(2,1)S(1)}, u32[]{:S(2)}, u32[]{:S(2)}) collective-permute-start(bf16[2,16,256]{2,1,0:T(8,128)(2,1)S(1)} %get-tuple-element.28), channel_id=1, source_target_pairs={{32,0},{33,1},{34,2},{35,3},{36,4},{37,5},{38,6},{39,7},{40,8},{41... | collective-permute-start | bytes 49160 | tf_op jit(solution)/shard_map/ppermute | solution.py:286
  11.1 1.4 %split.1 = (bf16[8,2,16,256]{3,2,1,0:T(8,128)(2,1)S(1)}, bf16[8,16,256]{2,1,0:T(8,128)(2,1)S(1)}, bf16[8,16,256]{2,1,0:T(8,128)(2,1)S(1)}) custom-call(bf16[8,2,256,256]{3,2,1,0:T(8,128)(2,1)S(1)} %get-tuple-element.24.refs_0_, bf16[8,2,16,256]{3,2,1,0:T(8,128)(2,1)S(1)} %get-tuple-element.25.refs_1_), custom_call_target="tpu_custom_call" | custom-call | tf_op jit(solution)/shard_map/split/pallas_call | solution.py:107
  12.6 0.1 inner_ahead.1
  12.6 0.0 collective-permute-done.right_in.refs_2_
  12.6 1.3 %collective-permute-start.1 = (bf16[8,16,256]{2,1,0:T(8,128)(2,1)S(1)}, bf16[8,16,256]{2,1,0:T(8,128)(2,1)S(1)}, u32[]{:S(2)}, u32[]{:S(2)}) collective-permute-start(bf16[8,16,256]{2,1,0:T(8,128)(2,1)S(1)} %get-tuple-element.31.refs_4_), channel_id=1, source_target_pairs={{1,0},{2,1},{3,2},{4,3},{5,4},{6,5},{7,6},{8,7},{9,8},{10,9},{11,1... | collective-permute-start | bytes 196616 | tf_op jit(solution)/shard_map/ppermute | solution.py:286
  13.9 2.1 %inner_near.1 = (bf16[4,2,256,256]{3,2,1,0:T(8,128)(2,1)}, f32[8,128]{1,0:T(8,128)S(1)}) custom-call(bf16[8,2,16,256]{3,2,1,0:T(8,128)(2,1)S(1)} %get-tuple-element.26.refs_0_, bf16[8,16,256]{2,1,0:T(8,128)(2,1)S(1)} %get-tuple-element.29.refs_1_, bf16[4,2,256,256]{3,2,1,0:T(8,128)(2,1)} %get-tuple-element.32.refs_2_, ...), custom_call_target="tpu_custom_call", output_to_operand_aliasing={{0}: (2, {})} | custom-call | tf_op jit(solution)/shard_map/inner_near/pallas_call | solution.py:241
  16.1 3.7 %collective-permute-done.1.refs_1_ = bf16[8,16,256]{2,1,0:T(8,128)(2,1)S(1)} collective-permute-done((bf16[8,16,256]{2,1,0:T(8,128)(2,1)S(1)}, bf16[8,16,256]{2,1,0:T(8,128)(2,1)S(1)}, u32[]{:S(2)}, u32[]{:S(2)}) %collective-permute-start.1) | collective-permute-done | bytes 65568 | tf_op jit(solution)/shard_map/ppermute | solution.py:286
  19.7 2.1 %outer.2 = (bf16[4,2,256,256]{3,2,1,0:T(8,128)(2,1)}, f32[2,4]{1,0:T(2,128)}, f32[2,4]{1,0:T(2,128)}, bf16[8,16,256]{2,1,0:T(8,128)(2,1)S(1)}) custom-call(bf16[8,2,16,256]{3,2,1,0:T(8,128)(2,1)S(1)} %get-tuple-element.26.refs_0_, bf16[8,16,256]{2,1,0:T(8,128)(2,1)S(1)} %collective-permute-done.1.refs_1_, ...), custom_call_target="tpu_custom_call", output_to_operand_aliasing={{3}: (4, {}), {0}: (5, {})} | custom-call | tf_op jit(solution)/shard_map/outer/pallas_call | solution.py:271
  21.9 1.3 %collective-permute-start.2 = (bf16[8,16,256]{2,1,0:T(8,128)(2,1)S(1)}, bf16[8,16,256]{2,1,0:T(8,128)(2,1)S(1)}, u32[]{:S(2)}, u32[]{:S(2)}) collective-permute-start(bf16[8,16,256]{2,1,0:T(8,128)(2,1)S(1)} %get-tuple-element.36.refs_4_), channel_id=1, source_target_pairs={{18,17},{19,18},{20,19},{21,20},{22,21},{23,22},{24,23},{25,24},{2... | collective-permute-start | bytes 196616 | tf_op jit(solution)/shard_map/ppermute | solution.py:286
  23.2 0.1 inner_far.1
  23.2 1.2 %collective-permute-done.2.refs_1_ = bf16[8,16,256]{2,1,0:T(8,128)(2,1)S(1)} collective-permute-done((bf16[8,16,256]{2,1,0:T(8,128)(2,1)S(1)}, bf16[8,16,256]{2,1,0:T(8,128)(2,1)S(1)}, u32[]{:S(2)}, u32[]{:S(2)}) %collective-permute-start.2) | collective-permute-done | bytes 65568 | tf_op jit(solution)/shard_map/ppermute | solution.py:286
  24.5 0.1 outer.3
  (1 shorter events, 0.0 us)
Async XLA Ops:
  2.4 10.3 %collective-permute-start = (bf16[2,16,256]{2,1,0:T(8,128)(2,1)S(1)}, bf16[2,16,256]{2,1,0:T(8,128)(2,1)S(1)}, u32[]{:S(2)}, u32[]{:S(2)}) collective-permute-start(bf16[2,16,256]{2,1,0:T(8,128)(2,1)S(1)} %get-tuple-element.28), channel_id=1, source_target_pairs={{32,0},{33,1},{34,2},{35,3},{36,4},{37,5},{38,6},{39,7},{40,8},{41... | collective-permute-start | bytes 49160 | tf_op jit(solution)/shard_map/ppermute | solution.py:286
  12.6 7.1 %collective-permute-start.1 = (bf16[8,16,256]{2,1,0:T(8,128)(2,1)S(1)}, bf16[8,16,256]{2,1,0:T(8,128)(2,1)S(1)}, u32[]{:S(2)}, u32[]{:S(2)}) collective-permute-start(bf16[8,16,256]{2,1,0:T(8,128)(2,1)S(1)} %get-tuple-element.31.refs_4_), channel_id=1, source_target_pairs={{1,0},{2,1},{3,2},{4,3},{5,4},{6,5},{7,6},{8,7},{9,8},{10,9},{11,1... | collective-permute-start | bytes 196616 | tf_op jit(solution)/shard_map/ppermute | solution.py:286
  21.9 2.6 %collective-permute-start.2 = (bf16[8,16,256]{2,1,0:T(8,128)(2,1)S(1)}, bf16[8,16,256]{2,1,0:T(8,128)(2,1)S(1)}, u32[]{:S(2)}, u32[]{:S(2)}) collective-permute-start(bf16[8,16,256]{2,1,0:T(8,128)(2,1)S(1)} %get-tuple-element.36.refs_4_), channel_id=1, source_target_pairs={{18,17},{19,18},{20,19},{21,20},{22,21},{23,22},{24,23},{25,24},{2... | collective-permute-start | bytes 196616 | tf_op jit(solution)/shard_map/ppermute | solution.py:286
